TPU v7x, 32 devices: a whole 2x2x4 slice. The times are simulated.
32 devices in a mesh: atoms: 4 (over y, x), energy: 8 (over z, core).
Axes of the slice: x: 2, y: 2, z: 4, core: 2. Of those that a mesh axis runs over, the one named last changes fastest.
Arguments:
- retarded_green_blocks: bfloat16 [4, 24, 2, 384, 384], P('atoms', 'energy'), may hold values from -0.21875 to 0.21875
- contact_lesser_sigma: bfloat16 [4, 24, 2, 384, 384], P('atoms', 'energy'), may hold values from -6 to 6
- energy_counts: int32 [8], replicated, may hold values from 1 to 3, 15 in all
- phonon_shift: int32 [64], replicated, may hold values from 1 to 7
- phonon_weight: float32 [4, 64], replicated, may hold values from 0.01 to 0.1
Outputs:
- scattered: bfloat16 [4, 24, 2, 384, 384], P('atoms', 'energy')
Inputs may be any that keep to these rules, and one draw needn't show every extreme that they name: energy_counts sums to 15; its largest entry is exactly 3.
All inputs are finite; a program needn't handle non-finite values.
Results may differ from a plain program's by a relative error of at most 0.007.
Values may be sent and summed in bfloat16 or wider, within the bound.
A program may use at most 64 MiB of HBM per device.

v0:
```python
import jax
import jax.numpy as jnp
from jax import lax
from jax.sharding import PartitionSpec as P


def extended(value, sides, width):
    for axis, dim in sides:
        size, length = (lax.axis_size(axis), value.shape[dim])
        up = [(i, (i + 1) % size) for i in range(size - 1)]
        down = [(j, i) for i, j in up]
        last = lax.slice_in_dim(value, length - width, length, axis=dim)
        leading = lax.slice_in_dim(value, 0, width, axis=dim)
        before = lax.ppermute(last, axis, up)
        after = lax.ppermute(leading, axis, down)
        value = jnp.concatenate([before, value, after], axis=dim)
    return value


def complex_product(left, right):
    prods = jnp.einsum("spik,sqkj->spqij", left, right, preferred_element_type=jnp.float32)
    return jnp.stack([prods[:, 0, 0] - prods[:, 1, 1], prods[:, 0, 1] + prods[:, 1, 0]], axis=1)


def product_adjoint(left, right):
    prods = jnp.einsum("spik,sqjk->spqij", left, right, preferred_element_type=jnp.float32)
    return jnp.stack([prods[:, 0, 0] + prods[:, 1, 1], prods[:, 1, 0] - prods[:, 0, 1]], axis=1)


def kernels(energy_counts, phonon_shift, phonon_weight, groups, per_group):
    total_slots = groups * per_group
    starts = jnp.cumsum(energy_counts) - energy_counts
    start_slot = jnp.broadcast_to(starts[:, None], (groups, per_group)).reshape(total_slots)
    slot_tally = jnp.broadcast_to(energy_counts[:, None], (groups, per_group)).reshape(total_slots)
    within = jnp.arange(total_slots, dtype=jnp.int32) % per_group
    energy_index = start_slot + within
    live = (within < slot_tally).astype(jnp.float32)
    spacing = energy_index[None, :] - energy_index[:, None]
    upward = (spacing[:, :, None] == phonon_shift[None, None, :]).astype(jnp.float32)
    downward = (spacing[:, :, None] == -phonon_shift[None, None, :]).astype(jnp.float32)
    mask = live[:, None] * live[None, :]
    own_kernel = jnp.sum(upward * phonon_weight[0] + downward * phonon_weight[1], axis=-1) * mask
    side_kernel = jnp.sum(upward * phonon_weight[2] + downward * phonon_weight[3], axis=-1) * mask
    return (own_kernel.astype(jnp.bfloat16), side_kernel.astype(jnp.bfloat16))


def on_device(
    retarded_green_blocks, contact_lesser_sigma, energy_counts, phonon_shift, phonon_weight
):
    groups = lax.axis_size("energy")
    per_group = retarded_green_blocks.shape[1]
    retarded = retarded_green_blocks[0]
    mixed = complex_product(retarded, contact_lesser_sigma[0]).astype(jnp.bfloat16)
    lesser = product_adjoint(mixed, retarded).astype(jnp.bfloat16)[None]
    own_kernel, side_kernel = kernels(energy_counts, phonon_shift, phonon_weight, groups, per_group)
    moved = lax.all_to_all(lesser, "energy", split_axis=3, concat_axis=1, tiled=True)
    regrouped = extended(moved, (("atoms", 0),), 1)
    slot_count = regrouped.shape[1]
    columns = regrouped.shape[2] * regrouped.shape[3] * regrouped.shape[4]
    flat = regrouped.reshape(3, slot_count, columns)
    sigma = jnp.dot(own_kernel, flat[1], preferred_element_type=jnp.float32)
    sigma = sigma + jnp.dot(side_kernel, flat[0], preferred_element_type=jnp.float32)
    sigma = sigma + jnp.dot(side_kernel, flat[2], preferred_element_type=jnp.float32)
    sigma = sigma.astype(jnp.bfloat16).reshape((1,) + regrouped.shape[1:])
    returned = lax.all_to_all(sigma, "energy", split_axis=1, concat_axis=3, tiled=True)
    result = complex_product(retarded, returned[0]).astype(jnp.bfloat16)
    return result[None]


def solution(mesh):
    in_specs = (
        P("atoms", "energy", None, None, None),
        P("atoms", "energy", None, None, None),
        P(),
        P(),
        P(),
    )
    out_specs = P("atoms", "energy", None, None, None)
    return jax.shard_map(
        on_device, mesh=mesh, in_specs=in_specs, out_specs=out_specs, check_vma=False
    )
```

profile of v0, /device:TPU:0, one launch (start us, length us, event | category | flops | bytes accessed | tf_op | source)
XLA Modules:
  0.0 195.5 jit_solution(2721880612030138604)
XLA Ops:
  0.0 1.5 copy-done
  1.5 3.6 %convolution_bitcast_fusion.2 = f32[3,2,2,384,384]{3,4,1,2,0:T(8,128)S(1)} fusion(bf16[1,3,2,384,384]{4,3,2,1,0:T(8,128)(2,1)} %param.6, bf16[1,3,2,384,384]{4,3,2,1,0:T(8,128)(2,1)S(1)} %copy-done), kind=kOutput, calls=%fused_computation.5 | convolution fusion | flops 1358954496 | bytes 10616832 | tf_op jit(solution)/shard_map/spik,sqkj->spqij/dot_general | solution.py:21
  5.3 0.2 fusion.15
  5.5 2.2 %convolution_bitcast_fusion.1 = f32[3,2,2,384,384]{4,3,2,1,0:T(8,128)S(1)} fusion(bf16[1,3,2,384,384]{4,3,2,1,0:T(8,128)(2,1)S(1)} %copy-done, bf16[3,1,384,384]{2,3,0,1:T(8,128)(2,1)S(1)} %fusion.16, bf16[3,1,384,384]{2,3,0,1:T(8,128)(2,1)S(1)} %fusion.15), kind=kOutput, calls=%fused_computation.4 | convolution fusion | flops 1359839232 | bytes 10616832 | tf_op jit(solution)/shard_map/spik,sqjk->spqij/dot_general | solution.py:26
  7.7 0.2 fusion.18
  8.1 0.2 pad_maximum_fusion
  8.3 1.8 copy.90
  10.1 48.2 %all_to_all.33 = bf16[1,3,2,384,384]{4,2,1,0,3:T(2,128)(2,1)S(1)} all-to-all(bf16[1,3,2,384,384]{4,2,1,0,3:T(2,128)(2,1)S(1)} %copy.90), channel_id=1, replica_groups=mesh['atoms'=4,'energy'=8] {'energy'}, dimensions={3} | all-to-all | bytes 3538944 | tf_op jit(solution)/shard_map/all_to_all | solution.py:56
  58.3 0.2 copy.91
  58.8 4.6 %collective-permute-start = (bf16[1,24,2,48,384]{4,3,2,1,0:T(8,128)(2,1)S(1)}, bf16[1,24,2,48,384]{4,3,2,1,0:T(8,128)(2,1)}, u32[]{:S(2)}, u32[]{:S(2)}) collective-permute-start(bf16[1,24,2,48,384]{4,3,2,1,0:T(8,128)(2,1)S(1)} %bitcast.119), channel_id=1, source_target_pairs={{0,8},{8,16},{16,24},{1,9},{9,17},{17,25},{2,10},{10,18},{18,26},{... | collective-permute-start | bytes 5308424 | tf_op jit(solution)/shard_map/ppermute | solution.py:14
  63.4 0.5 neg.4
  64.2 0.6 reshape.326
  64.8 0.7 reshape.327
  65.5 1.3 collective-permute-start.1
  66.8 0.6 fusion.31
  67.5 1.6 fusion.24
  69.1 0.7 compare_convert_fusion
  69.8 2.2 %squeeze.14 = bf16[24,36864]{1,0:T(8,128)(2,1)} reshape(bf16[1,8,3,2,48,384]{5,4,3,2,1,0:T(8,128)(2,1)S(1)} %copy.92) | data formatting | bytes 3538944 | tf_op jit(solution)/shard_map/squeeze | solution.py:61
  72.0 4.0 %fusion.27 = f32[24,36864]{1,0:T(8,128)} fusion(bf16[24,36864]{1,0:T(8,128)(2,1)} %squeeze.14, f32[24,24]{1,0:T(8,128)} %get-tuple-element.6, f32[24]{0:T(128)S(1)} %compare_convert_fusion), kind=kOutput, calls=%fused_computation.50 | convolution fusion | flops 42469056 | bytes 5310816 | tf_op jit(solution)/shard_map/dot_general | solution.py:61
  76.0 23.7 %collective-permute-done = bf16[1,24,2,48,384]{4,3,2,1,0:T(8,128)(2,1)} collective-permute-done((bf16[1,24,2,48,384]{4,3,2,1,0:T(8,128)(2,1)S(1)}, bf16[1,24,2,48,384]{4,3,2,1,0:T(8,128)(2,1)}, u32[]{:S(2)}, u32[]{:S(2)}) %collective-permute-start) | collective-permute-done | bytes 1769504 | tf_op jit(solution)/shard_map/ppermute | solution.py:14
  99.7 3.9 %squeeze.15 = bf16[24,36864]{1,0:T(8,128)(2,1)} reshape(bf16[1,24,2,48,384]{4,3,2,1,0:T(8,128)(2,1)} %collective-permute-done) | data formatting | bytes 3538944 | tf_op jit(solution)/shard_map/squeeze | solution.py:62
  103.7 5.0 %convolution_add_fusion.1 = f32[24,36864]{1,0:T(8,128)} fusion(f32[24,36864]{1,0:T(8,128)} %fusion.27, bf16[24,36864]{1,0:T(8,128)(2,1)} %squeeze.15, f32[24,24]{1,0:T(8,128)S(1)} %get-tuple-element.5, f32[24]{0:T(128)S(1)} %compare_convert_fusion), kind=kOutput, calls=%fused_computation.1 | convolution fusion | flops 43353792 | bytes 8849760 | tf_op jit(solution)/shard_map/dot_general | solution.py:62
  108.7 31.0 %collective-permute-done.1 = bf16[1,24,2,48,384]{4,3,2,1,0:T(8,128)(2,1)} collective-permute-done((bf16[1,24,2,48,384]{4,3,2,1,0:T(8,128)(2,1)S(1)}, bf16[1,24,2,48,384]{4,3,2,1,0:T(8,128)(2,1)}, u32[]{:S(2)}, u32[]{:S(2)}) %collective-permute-start.1) | collective-permute-done | bytes 1769504 | tf_op jit(solution)/shard_map/ppermute | solution.py:15
  139.7 2.7 %squeeze.16 = bf16[24,36864]{1,0:T(8,128)(2,1)S(1)} reshape(bf16[1,24,2,48,384]{4,3,2,1,0:T(8,128)(2,1)} %collective-permute-done.1) | data formatting | bytes 3538944 | tf_op jit(solution)/shard_map/squeeze | solution.py:63
  142.4 2.7 %fusion = bf16[24,36864]{1,0:T(8,128)(2,1)S(1)} fusion(f32[24,36864]{1,0:T(8,128)} %convolution_add_fusion.1, bf16[24,36864]{1,0:T(8,128)(2,1)S(1)} %squeeze.16, f32[24,24]{1,0:T(8,128)S(1)} %get-tuple-element.5, f32[24]{0:T(128)S(1)} %compare_convert_fusion), kind=kOutput, calls=%fused_computation.2 | convolution fusion | flops 44238528 | bytes 7080288 | tf_op jit(solution)/shard_map/dot_general | solution.py:63
  145.1 0.2 copy.116
  145.3 44.9 %all_to_all.34 = bf16[1,24,2,48,384]{4,3,2,0,1:T(8,128)(2,1)S(1)} all-to-all(bf16[1,24,2,48,384]{4,3,2,0,1:T(8,128)(2,1)S(1)} %bitcast.122), channel_id=1, replica_groups=mesh['atoms'=4,'energy'=8] {'energy'}, dimensions={1} | all-to-all | bytes 3538944 | tf_op jit(solution)/shard_map/all_to_all | solution.py:65
  190.2 0.2 copy.95
  190.4 2.2 %convolution_bitcast_fusion = f32[3,2,2,384,384]{3,4,1,2,0:T(8,128)S(1)} fusion(bf16[3,2,384,384,1]{3,2,4,1,0:T(8,128)(2,1)S(1)} %bitcast.125, bf16[1,3,2,384,384]{4,3,2,1,0:T(8,128)(2,1)S(1)} %copy-done), kind=kOutput, calls=%fused_computation.3 | convolution fusion | flops 1358954496 | bytes 10616832 | tf_op jit(solution)/shard_map/spik,sqkj->spqij/dot_general | solution.py:21
  192.8 0.2 fusion.19
  193.0 0.2 pad_maximum_fusion.1
  193.2 2.3 %copy.99 = bf16[1,3,2,384,384]{4,3,2,1,0:T(8,128)(2,1)} copy(bf16[1,3,2,384,384]{3,4,1,2,0:T(8,128)(2,1)S(1)} %pad_maximum_fusion.1) | data formatting | bytes 3538944 | tf_op jit(solution)/shard_map/stack | solution.py:22
  (17 shorter events, 1.1 us)
Async XLA Ops:
  0.0 1.5 copy-start
  58.5 4.9 %copy-start.2 = (s32[64]{0:T(128)S(1)}, s32[64]{0:T(128)}, u32[]{:S(2)}) copy-start(s32[64]{0:T(128)} %param.8) | copy-start | bytes 772
  58.6 5.4 %copy-start.3 = (s32[8]{0:T(128)S(1)}, s32[8]{0:T(128)}, u32[]{:S(2)}) copy-start(s32[8]{0:T(128)} %param.7) | copy-start | bytes 100
  58.6 8.8 %copy-start.1 = (f32[4,64]{1,0:T(4,128)S(1)}, f32[4,64]{1,0:T(4,128)}, u32[]{:S(2)}) copy-start(f32[4,64]{1,0:T(4,128)} %param.9) | copy-start | bytes 3076
  58.8 41.0 %collective-permute-start = (bf16[1,24,2,48,384]{4,3,2,1,0:T(8,128)(2,1)S(1)}, bf16[1,24,2,48,384]{4,3,2,1,0:T(8,128)(2,1)}, u32[]{:S(2)}, u32[]{:S(2)}) collective-permute-start(bf16[1,24,2,48,384]{4,3,2,1,0:T(8,128)(2,1)S(1)} %bitcast.119), channel_id=1, source_target_pairs={{0,8},{8,16},{16,24},{1,9},{9,17},{17,25},{2,10},{10,18},{18,26},{... | collective-permute-start | bytes 5308424 | tf_op jit(solution)/shard_map/ppermute | solution.py:14
  65.5 74.2 %collective-permute-start.1 = (bf16[1,24,2,48,384]{4,3,2,1,0:T(8,128)(2,1)S(1)}, bf16[1,24,2,48,384]{4,3,2,1,0:T(8,128)(2,1)}, u32[]{:S(2)}, u32[]{:S(2)}) collective-permute-start(bf16[1,24,2,48,384]{4,3,2,1,0:T(8,128)(2,1)S(1)} %bitcast.120), channel_id=1, source_target_pairs={{8,0},{16,8},{24,16},{9,1},{17,9},{25,17},{10,2},{18,10},{26,18},{... | collective-permute-start | bytes 5308424 | tf_op jit(solution)/shard_map/ppermute | solution.py:15
where the time goes:
time: 196 us; the launch traced here: 195 us
  blocking collectives  93 us (47%)
  waiting for transfers between devices  54.8 us (28%)
  matrix products  19.8 us (10%)
  local copies, waits for them, and re-layouts  16.6 us (8%)
  starting transfers between devices  5.92 us (3%)
  other arithmetic  5.25 us (3%)
    all_to_all x1, blocking collectives, on_device(): lax.all_to_all(lesser, 'energy', split_axis=3, concat_axis=1, tiled=True)  48.2 us
    all_to_all x1, blocking collectives, on_device(): lax.all_to_all(sigma, 'energy', split_axis=1, concat_axis=3, tiled=True)  44.9 us
    ppermute x1, waiting for transfers between devices, extended(): after = lax.ppermute(leading, axis, down)  31 us
    ppermute x1, waiting for transfers between devices, extended(): before = lax.ppermute(last, axis, up)  23.7 us
    dot_general x2, matrix products, complex_product(): jnp.einsum('spik,sqkj->spqij', left, right, preferred_element_type=jnp.fl...  5.83 us
    dot_general x1, matrix products, on_device(): jnp.dot(side_kernel, flat[0], preferred_element_type=jnp.float32)  5.02 us
    ppermute x1, starting transfers between devices, extended(): before = lax.ppermute(last, axis, up)  4.64 us
    dot_general x1, matrix products, on_device(): sigma = jnp.dot(own_kernel, flat[1], preferred_element_type=jnp.float32)  4.04 us
  transfers between devices with their start and end apart: 2, of which 2 were waited for; matrix products, arithmetic and copies ran while one was open for 10% of the time, Pallas kernels for 0%

commit v1 on v0

v1 whole, which is shorter than its diff:
```python
import functools

import jax
import jax.numpy as jnp
from jax import lax
from jax.experimental import pallas as pl
from jax.experimental.pallas import tpu as pltpu
from jax.sharding import PartitionSpec as P

TILE = 16
LANES = 128
MESH = pl.DeviceIdType.MESH


def coupling_tables(groups, per_group, counts_ref, shift_ref, weight_ref):
    rows = lax.broadcasted_iota(jnp.int32, (LANES, LANES), 0)
    lanes = lax.broadcasted_iota(jnp.int32, (LANES, LANES), 1)

    def slot_energy(index):
        energy = jnp.full((LANES, LANES), -1, jnp.int32)
        start = jnp.int32(0)
        for group in range(groups):
            count = counts_ref[group]
            for s in range(per_group):
                here = (index == group * per_group + s) & (s < count)
                energy = jnp.where(here, start + s, energy)
            start = start + count
        return energy

    energy_row = slot_energy(rows)
    energy_lane = slot_energy(lanes)
    own_space = energy_lane - energy_row
    side_space = energy_lane - rows

    def add(m, sums):
        own, side = sums
        shift = shift_ref[m]
        own = own + jnp.where(own_space == shift, weight_ref[0, m], 0.0)
        own = own + jnp.where(own_space == -shift, weight_ref[1, m], 0.0)
        side = side + jnp.where(side_space == shift, weight_ref[2, m], 0.0)
        side = side + jnp.where(side_space == -shift, weight_ref[3, m], 0.0)
        return own, side

    zero = jnp.zeros((LANES, LANES), jnp.float32)
    own, side = lax.fori_loop(0, shift_ref.shape[0], add, (zero, zero))
    own = jnp.where((energy_row >= 0) & (energy_lane >= 0), own, 0.0)
    side = jnp.where(energy_lane >= 0, side, 0.0)
    spread = jnp.where(energy_row == lanes, 1.0, 0.0)
    return own, side, spread


def spread_out(table, out_ref):
    height, width = out_ref.shape
    left_row = lax.broadcasted_iota(jnp.int32, (height, LANES), 0)
    left_lane = lax.broadcasted_iota(jnp.int32, (height, LANES), 1)
    left = jnp.where(left_row // TILE == left_lane, 1.0, 0.0).astype(jnp.bfloat16)
    right_row = lax.broadcasted_iota(jnp.int32, (LANES, width), 0)
    right_lane = lax.broadcasted_iota(jnp.int32, (LANES, width), 1)
    right = jnp.where(right_lane // TILE == right_row, 1.0, 0.0).astype(jnp.bfloat16)
    tall = jnp.dot(left, table.astype(jnp.bfloat16), preferred_element_type=jnp.float32)
    full = jnp.dot(tall.astype(jnp.bfloat16), right, preferred_element_type=jnp.float32)
    row = lax.broadcasted_iota(jnp.int32, (height, width), 0)
    lane = lax.broadcasted_iota(jnp.int32, (height, width), 1)
    out_ref[...] = jnp.where(row % TILE == lane % TILE, full, 0.0).astype(jnp.bfloat16)


def kernel(
    groups, blocks, counts_ref, shift_ref, weight_ref, r_ref, c_ref, o_ref,
    left, mixed, lesser, moved, own_mat, side_mat, spread_mat, side_part, below, above,
    sigma, back, total, send_a, recv_a, send_b, recv_b, local_a, local_b,
    send_up, recv_up, send_dn, recv_dn,
):
    per_group, _, orbitals, _ = r_ref.shape
    slots = groups * per_group
    chunks = moved.shape[0]
    depth = groups * TILE
    me = lax.axis_index("energy")
    block = lax.axis_index("atoms")
    has_below = block > 0
    has_above = block < blocks - 1

    barrier = pltpu.get_barrier_semaphore()
    for d in range(1, groups):
        pl.semaphore_signal(barrier, inc=1, device_id={"energy": lax.rem(me + d, groups)}, device_id_type=MESH)

    @pl.when(has_below)
    def _():
        pl.semaphore_signal(barrier, inc=1, device_id={"atoms": block - 1}, device_id_type=MESH)

    @pl.when(has_above)
    def _():
        pl.semaphore_signal(barrier, inc=1, device_id={"atoms": block + 1}, device_id_type=MESH)

    @pl.when(jnp.logical_not(has_below))
    def _():
        below[...] = jnp.zeros_like(below)

    @pl.when(jnp.logical_not(has_above))
    def _():
        above[...] = jnp.zeros_like(above)

    def complex_rows(dst, s, real, imag):
        dst[s, :orbitals, :orbitals] = real
        dst[s, :orbitals, orbitals:] = -imag
        dst[s, orbitals:, :orbitals] = imag
        dst[s, orbitals:, orbitals:] = real

    def mix(s, carry):
        complex_rows(left, s, r_ref[s, 0], r_ref[s, 1])
        contact = c_ref[s].reshape(2 * orbitals, orbitals)
        product = jnp.dot(left[s], contact, preferred_element_type=jnp.float32).astype(jnp.bfloat16)
        complex_rows(mixed, s, product[:orbitals], product[orbitals:])
        return carry

    lax.fori_loop(0, per_group, mix, 0)

    neighbours = jnp.where(has_below, 1, 0) + jnp.where(has_above, 1, 0)
    pl.semaphore_wait(barrier, groups - 1 + neighbours)

    def tile_rows(q, peer):
        return pl.ds(pl.multiple_of((q * groups + peer) * TILE, TILE), TILE)

    def out_copy(q, d):
        peer = lax.rem(me + d, groups)
        return pltpu.make_async_remote_copy(
            src_ref=lesser.at[:, tile_rows(q, peer), :],
            dst_ref=moved.at[q, pl.ds(me * per_group, per_group)],
            send_sem=send_a.at[q, d], recv_sem=recv_a.at[q, d],
            device_id={"energy": peer}, device_id_type=MESH,
        )

    def out_local(q):
        return pltpu.make_async_copy(
            lesser.at[:, tile_rows(q, me), :],
            moved.at[q, pl.ds(me * per_group, per_group)],
            local_a.at[q],
        )

    def back_copy(q, d):
        peer = lax.rem(me + d, groups)
        return pltpu.make_async_remote_copy(
            src_ref=sigma.at[q, pl.ds(peer * per_group, per_group)],
            dst_ref=back.at[:, tile_rows(q, me), :],
            send_sem=send_b.at[q, d], recv_sem=recv_b.at[q, d],
            device_id={"energy": peer}, device_id_type=MESH,
        )

    def back_local(q):
        return pltpu.make_async_copy(
            sigma.at[q, pl.ds(me * per_group, per_group)],
            back.at[:, tile_rows(q, me), :],
            local_b.at[q],
        )

    def up_copy(q):
        return pltpu.make_async_remote_copy(
            src_ref=side_part.at[q], dst_ref=below.at[q],
            send_sem=send_up.at[q], recv_sem=recv_up.at[q],
            device_id={"atoms": block + 1}, device_id_type=MESH,
        )

    def down_copy(q):
        return pltpu.make_async_remote_copy(
            src_ref=side_part.at[q], dst_ref=above.at[q],
            send_sem=send_dn.at[q], recv_sem=recv_dn.at[q],
            device_id={"atoms": block - 1}, device_id_type=MESH,
        )

    def send_lesser(q, carry):
        rows = pl.ds(pl.multiple_of(q * depth, depth), depth)
        for s in range(per_group):
            lesser[s, rows, :] = lax.dot_general(
                mixed[s, rows, :], left[s, :orbitals, :], (((1,), (1,)), ((), ())),
                preferred_element_type=jnp.float32,
            ).astype(jnp.bfloat16)
        for d in range(1, groups):
            out_copy(q, d).start()
        out_local(q).start()
        return carry

    lax.fori_loop(0, chunks, send_lesser, 0)

    own, side, spread = coupling_tables(groups, per_group, counts_ref, shift_ref, weight_ref)
    spread_out(own, own_mat)
    spread_out(side, side_mat)
    spread_out(spread, spread_mat)

    def send_side(q):
        for d in range(1, groups):
            out_copy(q, d).wait_recv()
        out_local(q).wait()
        values = moved[q].reshape(slots * TILE, orbitals)
        part = jnp.dot(side_mat[...], values, preferred_element_type=jnp.float32)
        side_part[q] = part.astype(jnp.bfloat16).reshape(side_part.shape[1:])

        @pl.when(has_above)
        def _():
            up_copy(q).start()

        @pl.when(has_below)
        def _():
            down_copy(q).start()

    def send_sigma(q):
        @pl.when(has_below)
        def _():
            up_copy(q).wait_recv()

        @pl.when(has_above)
        def _():
            down_copy(q).wait_recv()

        values = moved[q].reshape(slots * TILE, orbitals)
        flat = (side_mat.shape[0], orbitals)
        result = jnp.dot(own_mat[...], values, preferred_element_type=jnp.float32)
        result = result + jnp.dot(spread_mat[...], below[q].reshape(flat), preferred_element_type=jnp.float32)
        result = result + jnp.dot(spread_mat[...], above[q].reshape(flat), preferred_element_type=jnp.float32)
        sigma[q] = result.astype(jnp.bfloat16).reshape(sigma.shape[1:])
        for d in range(1, groups):
            back_copy(q, d).start()
        back_local(q).start()

    send_side(0)

    def middle(q, carry):
        send_side(q)
        send_sigma(q - 1)
        return carry

    lax.fori_loop(1, chunks, middle, 0)
    send_sigma(chunks - 1)

    def arrive(q, carry):
        for d in range(1, groups):
            back_copy(q, d).wait_recv()
        back_local(q).wait()
        return carry

    lax.fori_loop(0, chunks - 1, arrive, 0)
    cut = (chunks - 1) * depth

    def head(s, carry):
        total[s] = jnp.dot(left[s, :, :cut], back[s, :cut, :], preferred_element_type=jnp.float32)
        return carry

    lax.fori_loop(0, per_group, head, 0)
    arrive(chunks - 1, 0)

    def tail(s, carry):
        last = jnp.dot(left[s, :, cut:], back[s, cut:, :], preferred_element_type=jnp.float32)
        o_ref[s] = (total[s] + last).astype(jnp.bfloat16).reshape(2, orbitals, orbitals)
        return carry

    lax.fori_loop(0, per_group, tail, 0)

    def drain(q, carry):
        for d in range(1, groups):
            out_copy(q, d).wait_send()
            back_copy(q, d).wait_send()

        @pl.when(has_above)
        def _():
            up_copy(q).wait_send()

        @pl.when(has_below)
        def _():
            down_copy(q).wait_send()

        return carry

    lax.fori_loop(0, chunks, drain, 0)


def on_device(groups, blocks, retarded, contact, energy_counts, phonon_shift, phonon_weight):
    _, per_group, parts, orbitals, _ = retarded.shape
    slots = groups * per_group
    rows = parts * orbitals
    chunks = rows // (groups * TILE)
    energies = 2 * groups
    bf16, f32 = jnp.bfloat16, jnp.float32
    smem = pl.BlockSpec(memory_space=pltpu.SMEM)
    vmem = pl.BlockSpec(memory_space=pltpu.VMEM)
    dma = pltpu.SemaphoreType.DMA
    result = pl.pallas_call(
        functools.partial(kernel, groups, blocks),
        out_shape=jax.ShapeDtypeStruct(retarded.shape[1:], bf16),
        in_specs=[smem, smem, smem, vmem, vmem],
        out_specs=vmem,
        scratch_shapes=[
            pltpu.VMEM((per_group, rows, rows), bf16),
            pltpu.VMEM((per_group, rows, rows), bf16),
            pltpu.VMEM((per_group, rows, orbitals), bf16),
            pltpu.VMEM((chunks, slots, TILE, orbitals), bf16),
            pltpu.VMEM((slots * TILE, slots * TILE), bf16),
            pltpu.VMEM((energies * TILE, slots * TILE), bf16),
            pltpu.VMEM((slots * TILE, energies * TILE), bf16),
            pltpu.VMEM((chunks, energies, TILE, orbitals), bf16),
            pltpu.VMEM((chunks, energies, TILE, orbitals), bf16),
            pltpu.VMEM((chunks, energies, TILE, orbitals), bf16),
            pltpu.VMEM((chunks, slots, TILE, orbitals), bf16),
            pltpu.VMEM((per_group, rows, orbitals), bf16),
            pltpu.VMEM((per_group, rows, orbitals), f32),
            dma((chunks, groups)), dma((chunks, groups)),
            dma((chunks, groups)), dma((chunks, groups)),
            dma((chunks,)), dma((chunks,)),
            dma((chunks,)), dma((chunks,)), dma((chunks,)), dma((chunks,)),
        ],
        compiler_params=pltpu.CompilerParams(
            collective_id=0, has_side_effects=True, vmem_limit_bytes=60 << 20
        ),
    )(energy_counts, phonon_shift, phonon_weight, retarded[0], contact[0])
    return result[None]


def solution(mesh):
    split = P("atoms", "energy", None, None, None)
    return jax.shard_map(
        functools.partial(on_device, mesh.shape["energy"], mesh.shape["atoms"]),
        mesh=mesh, in_specs=(split, split, P(), P(), P()), out_specs=split, check_vma=False,
    )
```

time: 196 us -> 91.7 us (0.47)
  blocking collectives: 93 us -> 0 us
  Pallas kernels: 0 us -> 88.7 us
  waiting for transfers between devices: 54.8 us -> 0 us
  matrix products: 19.8 us -> 0 us
  local copies, waits for them, and re-layouts: 16.6 us -> 2.86 us
  starting transfers between devices: 5.92 us -> 0 us
  other arithmetic: 5.25 us -> 0 us
    all_to_all x2 -> x0, blocking collectives: 93 us -> none  [the longest x1 48.2 us: on_device(): lax.all_to_all(lesser, 'energy', split_axis=3, concat_axis=1, tiled=True)]
    pallas_call x0 -> x1, Pallas kernels: none -> 88.7 us  [on_device(): pl.pallas_call(functools.partial(kernel, groups, blocks), out_shape=jax.S...]
    ppermute x2 -> x0, waiting for transfers between devices: 54.8 us -> none  [the longest x1 31 us: extended(): after = lax.ppermute(leading, axis, down)]
    dot_general x6 -> x0, matrix products: 19.8 us -> none  [the longest x2 5.83 us: complex_product(): jnp.einsum('spik,sqkj->spqij', left, right, preferred_element_type=jnp.fl...]
    squeeze x3 -> x0, local copies, waits for them, and re-layouts: 8.78 us -> none  [the longest x1 3.91 us: on_device(): flat[0]]
    ppermute x2 -> x0, starting transfers between devices: 5.92 us -> none  [the longest x1 4.64 us: extended(): before = lax.ppermute(last, axis, up)]
    another operation x2 -> x0, local copies, waits for them, and re-layouts: 4.07 us -> none  [the longest x1 2.25 us: complex_product(): jnp.stack([prods[:, 0, 0] - prods[:, 1, 1], prods[:, 0, 1] + prods[:, 1,...]
  transfers between devices with their start and end apart: 2 -> 0, of which waited for: 2 -> 0; matrix products, arithmetic and copies ran while one was open for 10% -> 0% of each run, Pallas kernels for 0% -> 0%
where the time goes in v1:
time: 91.7 us; the launch traced here: 91.5 us
  Pallas kernels  88.7 us (97%)
  local copies, waits for them, and re-layouts  2.86 us (3%)
    pallas_call x1, Pallas kernels, on_device(): pl.pallas_call(functools.partial(kernel, groups, blocks), out_shape=jax.S...  88.7 us
    unnamed x1, local copies, waits for them, and re-layouts  2.86 us

profile of v1, /device:TPU:0, one launch (start us, length us, event | category | flops | bytes accessed | tf_op | source)
XLA Modules:
  0.0 91.5 jit_solution(18291533148840852814)
XLA Ops:
  0.0 88.7 %shard_map.55 = bf16[3,2,384,384]{3,2,1,0:T(8,128)(2,1)} custom-call(s32[8]{0:T(128)} %counts_ref.1, s32[64]{0:T(128)} %shift_ref.1, f32[4,64]{1,0:T(4,128)} %weight_ref.1, bf16[3,2,384,384]{3,2,1,0:T(8,128)(2,1)} %bitcast.4, bf16[3,2,384,384]{3,2,1,0:T(8,128)(2,1)} %bitcast.5), custom_call_target="tpu_custom_call" | custom-call | tf_op jit(solution)/shard_map/pallas_call | solution.py:284
  88.7 2.9 %copy.7 = bf16[1,3,2,384,384]{4,3,2,1,0:T(8,128)(2,1)} copy(bf16[1,3,2,384,384]{4,3,2,1,0:T(8,128)(2,1)} %bitcast.3) | data formatting | bytes 3538944

commit v2 on v1

--- a/solution.py
+++ b/solution.py
@@ -65,9 +65,10 @@
 
 
 def kernel(
-    groups, blocks, counts_ref, shift_ref, weight_ref, r_ref, c_ref, o_ref,
+    groups, blocks, light, counts_ref, shift_ref, weight_ref, r_ref, c_ref, o_ref,
     left, mixed, lesser, moved, own_mat, side_mat, spread_mat, side_part, below, above,
-    sigma, back, total, send_a, recv_a, send_b, recv_b, local_a, local_b,
+    sigma, back, total, send_f, recv_f, send_a, recv_a,
+    send_b, recv_b, local_a, local_b,
     send_up, recv_up, send_dn, recv_dn,
 ):
     per_group, _, orbitals, _ = r_ref.shape
@@ -99,20 +100,55 @@
     def _():
         above[...] = jnp.zeros_like(above)
 
-    def complex_rows(dst, s, real, imag):
-        dst[s, :orbitals, :orbitals] = real
-        dst[s, :orbitals, orbitals:] = -imag
-        dst[s, orbitals:, :orbitals] = imag
-        dst[s, orbitals:, orbitals:] = real
-
-    def mix(s, carry):
-        complex_rows(left, s, r_ref[s, 0], r_ref[s, 1])
-        contact = c_ref[s].reshape(2 * orbitals, orbitals)
-        product = jnp.dot(left[s], contact, preferred_element_type=jnp.float32).astype(jnp.bfloat16)
-        complex_rows(mixed, s, product[:orbitals], product[orbitals:])
-        return carry
-
-    lax.fori_loop(0, per_group, mix, 0)
+    for group in light:
+        for q in range(chunks):
+            moved[q, (group + 1) * per_group - 1] = jnp.zeros(moved.shape[2:], jnp.bfloat16)
+
+    def is_light(group):
+        flag = group < 0
+        for one in light:
+            flag = flag | (group == one)
+        return flag
+
+    def sized(group, act):
+        if not light:
+            act(per_group)
+            return
+        flag = is_light(group)
+        pl.when(flag)(lambda: act(per_group - 1))
+        pl.when(jnp.logical_not(flag))(lambda: act(per_group))
+
+    if light:
+        @pl.when(is_light(me))
+        def _():
+            back[per_group - 1] = jnp.zeros(back.shape[1:], jnp.bfloat16)
+
+    def complex_rows(dst, s, rows, lower, real, imag):
+        dst[s, rows, :orbitals] = real
+        dst[s, rows, orbitals:] = -imag
+        dst[s, lower, :orbitals] = imag
+        dst[s, lower, orbitals:] = real
+
+    def mix(s):
+        def copy_rows(i, carry):
+            at = pl.multiple_of(i * LANES, LANES)
+            rows, lower = pl.ds(at, LANES), pl.ds(at + orbitals, LANES)
+            complex_rows(left, s, rows, lower, r_ref[s, 0, rows, :], r_ref[s, 1, rows, :])
+            return carry
+
+        def mix_rows(i, carry):
+            at = pl.multiple_of(i * LANES, LANES)
+            rows, lower = pl.ds(at, LANES), pl.ds(at + orbitals, LANES)
+            contact = c_ref[s].reshape(2 * orbitals, orbitals)
+            real = jnp.dot(left[s, rows, :], contact, preferred_element_type=jnp.float32)
+            imag = jnp.dot(left[s, lower, :], contact, preferred_element_type=jnp.float32)
+            complex_rows(mixed, s, rows, lower, real.astype(jnp.bfloat16), imag.astype(jnp.bfloat16))
+            return carry
+
+        lax.fori_loop(0, orbitals // LANES, copy_rows, 0)
+        lax.fori_loop(0, orbitals // LANES, mix_rows, 0)
+
+    mix(0)
 
     neighbours = jnp.where(has_below, 1, 0) + jnp.where(has_above, 1, 0)
     pl.semaphore_wait(barrier, groups - 1 + neighbours)
@@ -120,37 +156,59 @@
     def tile_rows(q, peer):
         return pl.ds(pl.multiple_of((q * groups + peer) * TILE, TILE), TILE)
 
-    def out_copy(q, d):
+    def first_copy(q, d):
         peer = lax.rem(me + d, groups)
         return pltpu.make_async_remote_copy(
-            src_ref=lesser.at[:, tile_rows(q, peer), :],
-            dst_ref=moved.at[q, pl.ds(me * per_group, per_group)],
+            src_ref=lesser.at[pl.ds(0, 1), tile_rows(q, peer), :],
+            dst_ref=moved.at[q, pl.ds(me * per_group, 1)],
+            send_sem=send_f.at[q, d], recv_sem=recv_f.at[q, d],
+            device_id={"energy": peer}, device_id_type=MESH,
+        )
+
+    def out_copy(q, d, count):
+        peer = lax.rem(me + d, groups)
+        return pltpu.make_async_remote_copy(
+            src_ref=lesser.at[pl.ds(1, count - 1), tile_rows(q, peer), :],
+            dst_ref=moved.at[q, pl.ds(me * per_group + 1, count - 1)],
             send_sem=send_a.at[q, d], recv_sem=recv_a.at[q, d],
             device_id={"energy": peer}, device_id_type=MESH,
         )
 
-    def out_local(q):
+    def out_local(q, count):
         return pltpu.make_async_copy(
-            lesser.at[:, tile_rows(q, me), :],
-            moved.at[q, pl.ds(me * per_group, per_group)],
+            lesser.at[pl.ds(0, count), tile_rows(q, me), :],
+            moved.at[q, pl.ds(me * per_group, count)],
             local_a.at[q],
         )
 
-    def back_copy(q, d):
+    def back_copy(q, d, count):
         peer = lax.rem(me + d, groups)
         return pltpu.make_async_remote_copy(
-            src_ref=sigma.at[q, pl.ds(peer * per_group, per_group)],
-            dst_ref=back.at[:, tile_rows(q, me), :],
+            src_ref=sigma.at[q, pl.ds(peer * per_group, count)],
+            dst_ref=back.at[pl.ds(0, count), tile_rows(q, me), :],
             send_sem=send_b.at[q, d], recv_sem=recv_b.at[q, d],
             device_id={"energy": peer}, device_id_type=MESH,
         )
 
-    def back_local(q):
+    def back_local(q, count):
         return pltpu.make_async_copy(
-            sigma.at[q, pl.ds(me * per_group, per_group)],
-            back.at[:, tile_rows(q, me), :],
+            sigma.at[q, pl.ds(me * per_group, count)],
+            back.at[pl.ds(0, count), tile_rows(q, me), :],
             local_b.at[q],
         )
+
+    def each_peer(act):
+        def one(d, carry):
+            act(d)
+            return carry
+
+        lax.fori_loop(1, groups, one, 0)
+
+    def source(d):
+        return lax.rem(me + groups - d, groups)
+
+    def target(d):
+        return lax.rem(me + d, groups)
 
     def up_copy(q):
         return pltpu.make_async_remote_copy(
@@ -166,19 +224,42 @@
             device_id={"atoms": block - 1}, device_id_type=MESH,
         )
 
-    def send_lesser(q, carry):
+    def lesser_rows(q, first, last):
         rows = pl.ds(pl.multiple_of(q * depth, depth), depth)
-        for s in range(per_group):
+
+        def one(s, carry):
             lesser[s, rows, :] = lax.dot_general(
                 mixed[s, rows, :], left[s, :orbitals, :], (((1,), (1,)), ((), ())),
                 preferred_element_type=jnp.float32,
             ).astype(jnp.bfloat16)
-        for d in range(1, groups):
-            out_copy(q, d).start()
-        out_local(q).start()
-        return carry
-
-    lax.fori_loop(0, chunks, send_lesser, 0)
+            return carry
+
+        lax.fori_loop(first, last, one, 0)
+
+    def send_first(q, carry):
+        lesser_rows(q, 0, 1)
+        each_peer(lambda d: first_copy(q, d).start())
+        return carry
+
+    def send_rest(q, carry):
+        lesser_rows(q, 1, per_group)
+        sized(me, lambda n: each_peer(lambda d: out_copy(q, d, n).start()))
+        sized(me, lambda n: out_local(q, n).start())
+        return carry
+
+    def send_both(q, carry):
+        return send_rest(q, send_first(q, carry))
+
+    early = min(2, chunks)
+    lax.fori_loop(0, early, send_first, 0)
+
+    def mix_later(s, carry):
+        mix(s)
+        return carry
+
+    lax.fori_loop(1, per_group, mix_later, 0)
+    lax.fori_loop(0, early, send_rest, 0)
+    lax.fori_loop(early, chunks, send_both, 0)
 
     own, side, spread = coupling_tables(groups, per_group, counts_ref, shift_ref, weight_ref)
     spread_out(own, own_mat)
@@ -186,9 +267,12 @@
     spread_out(spread, spread_mat)
 
     def send_side(q):
-        for d in range(1, groups):
-            out_copy(q, d).wait_recv()
-        out_local(q).wait()
+        def got(d):
+            first_copy(q, d).wait_recv()
+            sized(source(d), lambda n: out_copy(q, d, n).wait_recv())
+
+        each_peer(got)
+        sized(me, lambda n: out_local(q, n).wait())
         values = moved[q].reshape(slots * TILE, orbitals)
         part = jnp.dot(side_mat[...], values, preferred_element_type=jnp.float32)
         side_part[q] = part.astype(jnp.bfloat16).reshape(side_part.shape[1:])
@@ -216,9 +300,8 @@
         result = result + jnp.dot(spread_mat[...], below[q].reshape(flat), preferred_element_type=jnp.float32)
         result = result + jnp.dot(spread_mat[...], above[q].reshape(flat), preferred_element_type=jnp.float32)
         sigma[q] = result.astype(jnp.bfloat16).reshape(sigma.shape[1:])
-        for d in range(1, groups):
-            back_copy(q, d).start()
-        back_local(q).start()
+        each_peer(lambda d: sized(target(d), lambda n: back_copy(q, d, n).start()))
+        sized(me, lambda n: back_local(q, n).start())
 
     send_side(0)
 
@@ -231,19 +314,24 @@
     send_sigma(chunks - 1)
 
     def arrive(q, carry):
-        for d in range(1, groups):
-            back_copy(q, d).wait_recv()
-        back_local(q).wait()
+        sized(me, lambda n: each_peer(lambda d: back_copy(q, d, n).wait_recv()))
+        sized(me, lambda n: back_local(q, n).wait())
         return carry
 
     lax.fori_loop(0, chunks - 1, arrive, 0)
     cut = (chunks - 1) * depth
 
-    def head(s, carry):
-        total[s] = jnp.dot(left[s, :, :cut], back[s, :cut, :], preferred_element_type=jnp.float32)
-        return carry
-
-    lax.fori_loop(0, per_group, head, 0)
+    row_blocks = 2 * orbitals // LANES
+
+    def block_rows(i):
+        return i // row_blocks, pl.ds(pl.multiple_of(lax.rem(i, row_blocks) * LANES, LANES), LANES)
+
+    def head(i, carry):
+        s, rows = block_rows(i)
+        total[s, rows, :] = jnp.dot(left[s, rows, :cut], back[s, :cut, :], preferred_element_type=jnp.float32)
+        return carry
+
+    lax.fori_loop(0, per_group * row_blocks, head, 0)
     arrive(chunks - 1, 0)
 
     def tail(s, carry):
@@ -254,9 +342,12 @@
     lax.fori_loop(0, per_group, tail, 0)
 
     def drain(q, carry):
-        for d in range(1, groups):
-            out_copy(q, d).wait_send()
-            back_copy(q, d).wait_send()
+        def gone(d):
+            first_copy(q, d).wait_send()
+            sized(me, lambda n: out_copy(q, d, n).wait_send())
+            sized(target(d), lambda n: back_copy(q, d, n).wait_send())
+
+        each_peer(gone)
 
         @pl.when(has_above)
         def _():
@@ -271,8 +362,8 @@
     lax.fori_loop(0, chunks, drain, 0)
 
 
-def on_device(groups, blocks, retarded, contact, energy_counts, phonon_shift, phonon_weight):
-    _, per_group, parts, orbitals, _ = retarded.shape
+def exchange(groups, blocks, light, identity, retarded, contact, energy_counts, phonon_shift, phonon_weight):
+    per_group, parts, orbitals, _ = retarded.shape
     slots = groups * per_group
     rows = parts * orbitals
     chunks = rows // (groups * TILE)
@@ -281,9 +372,9 @@
     smem = pl.BlockSpec(memory_space=pltpu.SMEM)
     vmem = pl.BlockSpec(memory_space=pltpu.VMEM)
     dma = pltpu.SemaphoreType.DMA
-    result = pl.pallas_call(
-        functools.partial(kernel, groups, blocks),
-        out_shape=jax.ShapeDtypeStruct(retarded.shape[1:], bf16),
+    return pl.pallas_call(
+        functools.partial(kernel, groups, blocks, light),
+        out_shape=jax.ShapeDtypeStruct(retarded.shape, bf16),
         in_specs=[smem, smem, smem, vmem, vmem],
         out_specs=vmem,
         scratch_shapes=[
@@ -300,16 +391,31 @@
             pltpu.VMEM((chunks, slots, TILE, orbitals), bf16),
             pltpu.VMEM((per_group, rows, orbitals), bf16),
             pltpu.VMEM((per_group, rows, orbitals), f32),
-            dma((chunks, groups)), dma((chunks, groups)),
-            dma((chunks, groups)), dma((chunks, groups)),
+            dma((chunks, groups)), dma((chunks, groups)), dma((chunks, groups)),
+            dma((chunks, groups)), dma((chunks, groups)), dma((chunks, groups)),
             dma((chunks,)), dma((chunks,)),
             dma((chunks,)), dma((chunks,)), dma((chunks,)), dma((chunks,)),
         ],
         compiler_params=pltpu.CompilerParams(
-            collective_id=0, has_side_effects=True, vmem_limit_bytes=60 << 20
+            collective_id=identity, has_side_effects=True, vmem_limit_bytes=40 << 20
         ),
-    )(energy_counts, phonon_shift, phonon_weight, retarded[0], contact[0])
-    return result[None]
+    )(energy_counts, phonon_shift, phonon_weight, retarded, contact)
+
+
+LIGHT = False
+
+
+def on_device(groups, blocks, retarded, contact, energy_counts, phonon_shift, phonon_weight):
+    operands = (retarded[0], contact[0], energy_counts, phonon_shift, phonon_weight)
+    if not LIGHT:
+        return exchange(groups, blocks, (), 0, *operands)[None]
+    pairs = groups // 2
+    full = (energy_counts == retarded.shape[1]).reshape(pairs, 2).any(axis=1)
+    chosen = jnp.argmin(full.astype(jnp.int32))
+    branches = [
+        functools.partial(exchange, groups, blocks, (2 * pair, 2 * pair + 1), pair) for pair in range(pairs)
+    ]
+    return lax.switch(chosen, branches, *operands)[None]
 
 
 def solution(mesh):

time: 91.7 us -> 93.7 us (1.022)
  local copies, waits for them, and re-layouts: 2.86 us -> 6.15 us
  Pallas kernels: 88.7 us -> 87.2 us
    unnamed x1 -> x11, local copies, waits for them, and re-layouts: 2.86 us -> 6.15 us
    pallas_call x1, Pallas kernels: 88.7 us -> 87.2 us  [exchange(): pl.pallas_call(functools.partial(kernel, groups, blocks, light), out_shap...]
where the time goes in v2:
time: 93.7 us; the launch traced here: 93.4 us
  Pallas kernels  87.2 us (93%)
  local copies, waits for them, and re-layouts  6.15 us (7%)
    pallas_call x1, Pallas kernels, exchange(): pl.pallas_call(functools.partial(kernel, groups, blocks, light), out_shap...  87.2 us
    unnamed x11, local copies, waits for them, and re-layouts  6.15 us

profile of v2, /device:TPU:0, one launch (start us, length us, event | category | flops | bytes accessed | tf_op | source)
XLA Modules:
  0.0 93.4 jit_solution(1870520715024173297)
XLA Ops:
  0.0 0.0 copy-start
  0.0 1.5 %copy-done = bf16[1,3,2,384,384]{4,3,2,1,0:T(8,128)(2,1)S(1)} copy-done((bf16[1,3,2,384,384]{4,3,2,1,0:T(8,128)(2,1)S(1)}, bf16[1,3,2,384,384]{4,3,2,1,0:T(8,128)(2,1)}, u32[]{:S(2)}) %copy-start) | copy-done | bytes 1769496
  1.5 0.0 copy-start.1
  1.5 1.5 %copy-done.1 = bf16[1,3,2,384,384]{4,3,2,1,0:T(8,128)(2,1)S(1)} copy-done((bf16[1,3,2,384,384]{4,3,2,1,0:T(8,128)(2,1)S(1)}, bf16[1,3,2,384,384]{4,3,2,1,0:T(8,128)(2,1)}, u32[]{:S(2)}) %copy-start.1) | copy-done | bytes 1769496
  3.0 0.0 copy-start.2
  3.0 0.7 copy-done.2
  3.6 0.0 copy-start.3
  3.6 0.7 copy-done.3
  4.3 0.0 copy-start.4
  4.3 0.7 copy-done.4
  4.9 87.2 %shard_map.55 = bf16[3,2,384,384]{3,2,1,0:T(8,128)(2,1)S(1)} custom-call(s32[8]{0:T(128)S(1)} %copy-done.3, s32[64]{0:T(128)S(1)} %copy-done.4, f32[4,64]{1,0:T(4,128)S(1)} %copy-done.2, bf16[3,2,384,384]{3,2,1,0:T(8,128)(2,1)S(1)} %bitcast.4, bf16[3,2,384,384]{3,2,1,0:T(8,128)(2,1)S(1)} %bitcast.5), custom_call_target="tpu_custom_call" | custom-call | tf_op jit(solution)/shard_map/pallas_call | solution.py:375
  92.2 1.2 %copy.7 = bf16[1,3,2,384,384]{4,3,2,1,0:T(8,128)(2,1)} copy(bf16[1,3,2,384,384]{4,3,2,1,0:T(8,128)(2,1)S(1)} %bitcast.3) | data formatting | bytes 3538944
Async XLA Ops:
  0.0 1.5 %copy-start = (bf16[1,3,2,384,384]{4,3,2,1,0:T(8,128)(2,1)S(1)}, bf16[1,3,2,384,384]{4,3,2,1,0:T(8,128)(2,1)}, u32[]{:S(2)}) copy-start(bf16[1,3,2,384,384]{4,3,2,1,0:T(8,128)(2,1)} %param.5) | copy-start | bytes 5308420
  1.5 1.5 %copy-start.1 = (bf16[1,3,2,384,384]{4,3,2,1,0:T(8,128)(2,1)S(1)}, bf16[1,3,2,384,384]{4,3,2,1,0:T(8,128)(2,1)}, u32[]{:S(2)}) copy-start(bf16[1,3,2,384,384]{4,3,2,1,0:T(8,128)(2,1)} %param.6) | copy-start | bytes 5308420
  3.0 0.7 copy-start.2
  3.6 0.7 copy-start.3
  4.3 0.7 copy-start.4

commit v3 on v2

--- a/solution.py
+++ b/solution.py
@@ -402,7 +402,7 @@
     )(energy_counts, phonon_shift, phonon_weight, retarded, contact)
 
 
-LIGHT = False
+LIGHT = True
 
 
 def on_device(groups, blocks, retarded, contact, energy_counts, phonon_shift, phonon_weight):

time: 93.7 us -> 87.7 us (0.936)
  local copies, waits for them, and re-layouts: 6.15 us -> 1.3 us
  Pallas kernels: 87.2 us -> 83 us
  other arithmetic: 0 us -> 1.51 us
    unnamed x11 -> x1, local copies, waits for them, and re-layouts: 6.15 us -> 1.21 us
    pallas_call x1, Pallas kernels: 87.2 us -> 83 us  [exchange(): pl.pallas_call(functools.partial(kernel, groups, blocks, light), out_shap...]
where the time goes in v3:
time: 87.7 us; the launch traced here: 86.8 us
  Pallas kernels  83 us (95%)
  other arithmetic  1.51 us (2%)
  local copies, waits for them, and re-layouts  1.3 us (1%)
    pallas_call x1, Pallas kernels, exchange(): pl.pallas_call(functools.partial(kernel, groups, blocks, light), out_shap...  83 us

profile of v3, /device:TPU:0, one launch (start us, length us, event | category | flops | bytes accessed | tf_op | source)
XLA Modules:
  0.0 86.8 jit_solution(9108025567669812262)
XLA Ops:
  0.0 0.7 broadcast_compare_fusion
  0.7 0.1 reshape.3
  0.7 0.1 reduce_or.9
  0.9 0.7 iota_reduce_fusion
  2.3 83.3 %conditional.1 = (bf16[1,3,2,384,384]{4,3,2,1,0:T(8,128)(2,1)S(1)}) conditional(s32[]{:T(128)} %clamp.3, (s32[8]{0:T(128)}, s32[64]{0:T(128)}, f32[4,64]{1,0:T(4,128)}, bf16[1,3,2,384,384]{4,3,2,1,0:T(8,128)(2,1)}, bf16[1,3,2,384,384]{4,3,2,1,0:T(8,128)(2,1)}) %tuple.23, (s32[8]{0:T(128)}, s32[64]{0:T(128)}, ...), branch_computations={%region_2.3_spmd, %region_3.4_spmd, %region_4.5_spmd, %region_5.6_... | conditional | bytes 8 | solution.py:418
  2.3 83.0 %branch_1_fun.1 = bf16[3,2,384,384]{3,2,1,0:T(8,128)(2,1)S(1)} custom-call(s32[8]{0:T(128)} %get-tuple-element.56.counts_ref, s32[64]{0:T(128)} %get-tuple-element.91.shift_ref, f32[4,64]{1,0:T(4,128)} %get-tuple-element.95.weight_ref, bf16[3,2,384,384]{3,2,1,0:T(8,128)(2,1)} %bitcast.13, bf16[3,2,384,384]{3,2,1,0:T(8,128)(2,1)} %bitcast.17), custom_call_target="tpu_custom_call" | custom-call | tf_op jit(solution)/shard_map/cond/branch_1_fun/pallas_call | solution.py:375
  85.6 1.2 %copy.31 = bf16[1,3,2,384,384]{4,3,2,1,0:T(8,128)(2,1)} copy(bf16[1,3,2,384,384]{4,3,2,1,0:T(8,128)(2,1)S(1)} %get-tuple-element.73) | data formatting | bytes 3538944

commit v4 on v3

--- a/solution.py
+++ b/solution.py
@@ -1,7 +1,9 @@
 import functools
+import itertools
 
 import jax
 import jax.numpy as jnp
+import numpy as np
 from jax import lax
 from jax.experimental import pallas as pl
 from jax.experimental.pallas import tpu as pltpu
@@ -9,6 +11,7 @@
 
 TILE = 16
 LANES = 128
+LIGHT = 3
 MESH = pl.DeviceIdType.MESH
 
 
@@ -51,27 +54,34 @@
 
 def spread_out(table, out_ref):
     height, width = out_ref.shape
-    left_row = lax.broadcasted_iota(jnp.int32, (height, LANES), 0)
-    left_lane = lax.broadcasted_iota(jnp.int32, (height, LANES), 1)
-    left = jnp.where(left_row // TILE == left_lane, 1.0, 0.0).astype(jnp.bfloat16)
     right_row = lax.broadcasted_iota(jnp.int32, (LANES, width), 0)
     right_lane = lax.broadcasted_iota(jnp.int32, (LANES, width), 1)
     right = jnp.where(right_lane // TILE == right_row, 1.0, 0.0).astype(jnp.bfloat16)
-    tall = jnp.dot(left, table.astype(jnp.bfloat16), preferred_element_type=jnp.float32)
-    full = jnp.dot(tall.astype(jnp.bfloat16), right, preferred_element_type=jnp.float32)
-    row = lax.broadcasted_iota(jnp.int32, (height, width), 0)
-    lane = lax.broadcasted_iota(jnp.int32, (height, width), 1)
-    out_ref[...] = jnp.where(row % TILE == lane % TILE, full, 0.0).astype(jnp.bfloat16)
+    wide = jnp.dot(table.astype(jnp.bfloat16), right, preferred_element_type=jnp.float32).astype(jnp.bfloat16)
+
+    def some_rows(i, carry):
+        at = pl.multiple_of(i * LANES, LANES)
+        left_row = lax.broadcasted_iota(jnp.int32, (LANES, LANES), 0) + at
+        left_lane = lax.broadcasted_iota(jnp.int32, (LANES, LANES), 1)
+        left = jnp.where(left_row // TILE == left_lane, 1.0, 0.0).astype(jnp.bfloat16)
+        full = jnp.dot(left, wide, preferred_element_type=jnp.float32)
+        out_ref[pl.ds(at, LANES), :] = jnp.where(
+            right_row % TILE == right_lane % TILE, full, 0.0
+        ).astype(jnp.bfloat16)
+        return carry
+
+    lax.fori_loop(0, height // LANES, some_rows, 0)
 
 
 def kernel(
-    groups, blocks, light, counts_ref, shift_ref, weight_ref, r_ref, c_ref, o_ref,
+    groups, blocks, light, counts_ref, shift_ref, weight_ref, r_hbm, c_hbm, o_ref,
+    r_ref, c_ref, load_r, load_c,
     left, mixed, lesser, moved, own_mat, side_mat, spread_mat, side_part, below, above,
     sigma, back, total, send_f, recv_f, send_a, recv_a,
     send_b, recv_b, local_a, local_b,
     send_up, recv_up, send_dn, recv_dn,
 ):
-    per_group, _, orbitals, _ = r_ref.shape
+    per_group, _, orbitals, _ = r_hbm.shape
     slots = groups * per_group
     chunks = moved.shape[0]
     depth = groups * TILE
@@ -80,6 +90,16 @@
     has_below = block > 0
     has_above = block < blocks - 1
 
+    def load(s):
+        return (
+            pltpu.make_async_copy(r_hbm.at[s], r_ref.at[s], load_r.at[s]),
+            pltpu.make_async_copy(c_hbm.at[s], c_ref.at[s], load_c.at[s]),
+        )
+
+    for s in range(per_group):
+        for copy in load(s):
+            copy.start()
+
     barrier = pltpu.get_barrier_semaphore()
     for d in range(1, groups):
         pl.semaphore_signal(barrier, inc=1, device_id={"energy": lax.rem(me + d, groups)}, device_id_type=MESH)
@@ -145,6 +165,8 @@
             complex_rows(mixed, s, rows, lower, real.astype(jnp.bfloat16), imag.astype(jnp.bfloat16))
             return carry
 
+        for copy in load(s):
+            copy.wait()
         lax.fori_loop(0, orbitals // LANES, copy_rows, 0)
         lax.fori_loop(0, orbitals // LANES, mix_rows, 0)
 
@@ -247,8 +269,12 @@
         sized(me, lambda n: out_local(q, n).start())
         return carry
 
-    def send_both(q, carry):
-        return send_rest(q, send_first(q, carry))
+    def send_later(q, carry):
+        @pl.when(q >= early)
+        def _():
+            send_first(q, 0)
+
+        return send_rest(q, carry)
 
     early = min(2, chunks)
     lax.fori_loop(0, early, send_first, 0)
@@ -258,8 +284,7 @@
         return carry
 
     lax.fori_loop(1, per_group, mix_later, 0)
-    lax.fori_loop(0, early, send_rest, 0)
-    lax.fori_loop(early, chunks, send_both, 0)
+    lax.fori_loop(0, chunks, send_later, 0)
 
     own, side, spread = coupling_tables(groups, per_group, counts_ref, shift_ref, weight_ref)
     spread_out(own, own_mat)
@@ -273,9 +298,15 @@
 
         each_peer(got)
         sized(me, lambda n: out_local(q, n).wait())
-        values = moved[q].reshape(slots * TILE, orbitals)
-        part = jnp.dot(side_mat[...], values, preferred_element_type=jnp.float32)
-        side_part[q] = part.astype(jnp.bfloat16).reshape(side_part.shape[1:])
+        def some_rows(i, carry):
+            rows = pl.ds(pl.multiple_of(i * LANES, LANES), LANES)
+            values = moved[q].reshape(slots * TILE, orbitals)
+            part = jnp.dot(side_mat[rows, :], values, preferred_element_type=jnp.float32)
+            tiles = pl.ds(i * (LANES // TILE), LANES // TILE)
+            side_part[q, tiles] = part.astype(jnp.bfloat16).reshape(LANES // TILE, TILE, orbitals)
+            return carry
+
+        lax.fori_loop(0, side_mat.shape[0] // LANES, some_rows, 0)
 
         @pl.when(has_above)
         def _():
@@ -294,24 +325,35 @@
         def _():
             down_copy(q).wait_recv()
 
-        values = moved[q].reshape(slots * TILE, orbitals)
         flat = (side_mat.shape[0], orbitals)
-        result = jnp.dot(own_mat[...], values, preferred_element_type=jnp.float32)
-        result = result + jnp.dot(spread_mat[...], below[q].reshape(flat), preferred_element_type=jnp.float32)
-        result = result + jnp.dot(spread_mat[...], above[q].reshape(flat), preferred_element_type=jnp.float32)
-        sigma[q] = result.astype(jnp.bfloat16).reshape(sigma.shape[1:])
+
+        def some_rows(i, carry):
+            rows = pl.ds(pl.multiple_of(i * LANES, LANES), LANES)
+            values = moved[q].reshape(slots * TILE, orbitals)
+            result = jnp.dot(own_mat[rows, :], values, preferred_element_type=jnp.float32)
+            spread = spread_mat[rows, :]
+            result = result + jnp.dot(spread, below[q].reshape(flat), preferred_element_type=jnp.float32)
+            result = result + jnp.dot(spread, above[q].reshape(flat), preferred_element_type=jnp.float32)
+            tiles = pl.ds(i * (LANES // TILE), LANES // TILE)
+            sigma[q, tiles] = result.astype(jnp.bfloat16).reshape(LANES // TILE, TILE, orbitals)
+            return carry
+
+        lax.fori_loop(0, own_mat.shape[0] // LANES, some_rows, 0)
         each_peer(lambda d: sized(target(d), lambda n: back_copy(q, d, n).start()))
         sized(me, lambda n: back_local(q, n).start())
 
-    send_side(0)
-
     def middle(q, carry):
-        send_side(q)
-        send_sigma(q - 1)
-        return carry
-
-    lax.fori_loop(1, chunks, middle, 0)
-    send_sigma(chunks - 1)
+        @pl.when(q < chunks)
+        def _():
+            send_side(q)
+
+        @pl.when(q > 0)
+        def _():
+            send_sigma(q - 1)
+
+        return carry
+
+    lax.fori_loop(0, chunks + 1, middle, 0)
 
     def arrive(q, carry):
         sized(me, lambda n: each_peer(lambda d: back_copy(q, d, n).wait_recv()))
@@ -371,13 +413,17 @@
     bf16, f32 = jnp.bfloat16, jnp.float32
     smem = pl.BlockSpec(memory_space=pltpu.SMEM)
     vmem = pl.BlockSpec(memory_space=pltpu.VMEM)
+    hbm = pl.BlockSpec(memory_space=pl.ANY)
     dma = pltpu.SemaphoreType.DMA
     return pl.pallas_call(
         functools.partial(kernel, groups, blocks, light),
         out_shape=jax.ShapeDtypeStruct(retarded.shape, bf16),
-        in_specs=[smem, smem, smem, vmem, vmem],
+        in_specs=[smem, smem, smem, hbm, hbm],
         out_specs=vmem,
         scratch_shapes=[
+            pltpu.VMEM(retarded.shape, bf16),
+            pltpu.VMEM(retarded.shape, bf16),
+            dma((per_group,)), dma((per_group,)),
             pltpu.VMEM((per_group, rows, rows), bf16),
             pltpu.VMEM((per_group, rows, rows), bf16),
             pltpu.VMEM((per_group, rows, orbitals), bf16),
@@ -397,23 +443,33 @@
             dma((chunks,)), dma((chunks,)), dma((chunks,)), dma((chunks,)),
         ],
         compiler_params=pltpu.CompilerParams(
-            collective_id=identity, has_side_effects=True, vmem_limit_bytes=40 << 20
+            collective_id=identity, has_side_effects=True, vmem_limit_bytes=58 << 20
         ),
     )(energy_counts, phonon_shift, phonon_weight, retarded, contact)
 
 
-LIGHT = True
+def light_sets(groups):
+    if groups > 8:
+        return [(group, group + 1) for group in range(0, groups, 2)]
+    left = set(itertools.combinations(range(groups), (groups - 1) // 2))
+    options = list(itertools.combinations(range(groups), LIGHT))
+    family = []
+    while left:
+        best = max(options, key=lambda option: sum(not set(option) & set(full) for full in left))
+        family.append(best)
+        left = {full for full in left if set(best) & set(full)}
+    return family
 
 
 def on_device(groups, blocks, retarded, contact, energy_counts, phonon_shift, phonon_weight):
     operands = (retarded[0], contact[0], energy_counts, phonon_shift, phonon_weight)
-    if not LIGHT:
-        return exchange(groups, blocks, (), 0, *operands)[None]
-    pairs = groups // 2
-    full = (energy_counts == retarded.shape[1]).reshape(pairs, 2).any(axis=1)
-    chosen = jnp.argmin(full.astype(jnp.int32))
+    family = light_sets(groups)
+    member = np.array([[group in one for group in range(groups)] for one in family], np.float32)
+    full = (energy_counts == retarded.shape[1]).astype(jnp.float32)
+    clashes = jnp.sum(member * full[None, :], axis=1)
+    chosen = jnp.argmin(clashes)
     branches = [
-        functools.partial(exchange, groups, blocks, (2 * pair, 2 * pair + 1), pair) for pair in range(pairs)
+        functools.partial(exchange, groups, blocks, one, identity) for identity, one in enumerate(family)
     ]
     return lax.switch(chosen, branches, *operands)[None]
 

time: 87.7 us -> 88.5 us (level)
  no operation moved by 1% of the time
where the time goes in v4:
time: 88.5 us; the launch traced here: 87.6 us
  Pallas kernels  83 us (94%)
  other arithmetic  2.16 us (2%)
  local copies, waits for them, and re-layouts  1.21 us (1%)
    pallas_call x1, Pallas kernels, exchange(): pl.pallas_call(functools.partial(kernel, groups, blocks, light), out_shap...  83 us

profile of v4, /device:TPU:0, one launch (start us, length us, event | category | flops | bytes accessed | tf_op | source)
XLA Modules:
  0.0 87.6 jit_solution(8273033745853747204)
XLA Ops:
  0.0 0.7 compare_convert_fusion
  0.7 0.8 multiply_reduce_fusion
  1.4 0.7 iota_reduce_fusion
  2.9 83.6 %conditional.1 = (bf16[1,3,2,384,384]{4,3,2,1,0:T(8,128)(2,1)S(1)}) conditional(s32[]{:T(128)} %clamp.3, (s32[8]{0:T(128)}, s32[64]{0:T(128)}, f32[4,64]{1,0:T(4,128)}, bf16[1,3,2,384,384]{4,3,2,1,0:T(8,128)(2,1)}, bf16[1,3,2,384,384]{4,3,2,1,0:T(8,128)(2,1)}) %tuple.43, (s32[8]{0:T(128)}, s32[64]{0:T(128)}, ...), branch_computations={%region_2.3_spmd, %region_3.4_spmd, %region_4.5_spmd, %region_5.6_... | conditional | bytes 8 | solution.py:474
  2.9 83.0 %branch_0_fun.1 = bf16[3,2,384,384]{3,2,1,0:T(8,128)(2,1)S(1)} custom-call(s32[8]{0:T(128)} %get-tuple-element.98.counts_ref, s32[64]{0:T(128)} %get-tuple-element.190.shift_ref, f32[4,64]{1,0:T(4,128)} %get-tuple-element.199.weight_ref, bf16[3,2,384,384]{3,2,1,0:T(8,128)(2,1)} %bitcast.27, bf16[3,2,384,384]{3,2,1,0:T(8,128)(2,1)} %bitcast.36), custom_call_target="tpu_custom_call" | custom-call | tf_op jit(solution)/shard_map/cond/branch_0_fun/pallas_call | solution.py:418
  86.4 1.2 %copy.62 = bf16[1,3,2,384,384]{4,3,2,1,0:T(8,128)(2,1)} copy(bf16[1,3,2,384,384]{4,3,2,1,0:T(8,128)(2,1)S(1)} %get-tuple-element.153) | data formatting | bytes 3538944
